TPU v7x, 32 devices: a whole 2x2x4 slice. The times are simulated.
32 devices in a mesh: group: 4 (over y, core), freq: 8 (over z, x).
Axes of the slice: x: 2, y: 2, z: 4, core: 2. Of those that a mesh axis runs over, the one named last changes fastest.
Arguments:
- spectra: bfloat16 [2048, 2, 16], P('freq', None, 'group'), may hold values from -6 to 6
- templates: bfloat16 [2048, 2, 2560], P('freq', None, 'group'), may hold values from -600 to 600
- valid_start: int32 [16], replicated, may hold values from 0 to 2048
Outputs:
- peaks: float32 [2560, 16], P('group')
All inputs are finite; a program needn't handle non-finite values.
Results may differ from a plain program's by a relative error of at most 0.0019.
Values may be sent and summed in bfloat16 or wider, within the bound.
A program may use at most 256 MiB of HBM per device.

v0:
```python
import math

import jax
import jax.numpy as jnp
from jax import lax
from jax.sharding import PartitionSpec as P

N = 4096
VALID = 2048


def make_table(bins_count, lag_index):
    bins_index = jnp.arange(bins_count, dtype=jnp.int32)
    angle = (bins_index[:, None] * lag_index[None, :] % N).astype(jnp.float32) * (2.0 * math.pi / N)
    cosine = jnp.cos(angle)
    sine_part = jnp.sin(angle)
    upper = jnp.concatenate([cosine, sine_part], 1)
    lower = jnp.concatenate([-sine_part, cosine], 1)
    return jnp.concatenate([upper, lower], 0).astype(jnp.bfloat16)


def make_cross(bank_piece, seg_piece):
    bank_re = bank_piece[:, 0, :].astype(jnp.float32)[:, None, :]
    bank_im = bank_piece[:, 1, :].astype(jnp.float32)[:, None, :]
    seg_re = seg_piece[:, 0, :].astype(jnp.float32)[:, :, None]
    seg_im = seg_piece[:, 1, :].astype(jnp.float32)[:, :, None]
    cross_re = bank_re * seg_re + bank_im * seg_im
    cross_im = bank_re * seg_im - bank_im * seg_re
    joined = jnp.stack([cross_re, cross_im], 0).astype(jnp.bfloat16)
    return joined.reshape(2 * joined.shape[1], joined.shape[2] * joined.shape[3])


def contract(cross, table):
    return lax.dot_general(
        cross, table, (((0,), (0,)), ((), ())), preferred_element_type=jnp.float32
    )


def on_device(spectra, templates, valid_start):
    freq_count = lax.axis_size("freq")
    lag_count = N // freq_count
    lag_index = lax.axis_index("freq") * lag_count + jnp.arange(lag_count, dtype=jnp.int32)
    tpl_rows = templates.shape[2]
    every_segment = lax.all_gather(spectra, "group", axis=2, tiled=True)
    count = every_segment.shape[2]
    bank_piece = lax.all_gather(templates, "freq", axis=0, tiled=True)
    seg_piece = lax.all_gather(every_segment, "freq", axis=0, tiled=True)
    width = bank_piece.shape[0]
    cross = make_cross(bank_piece, seg_piece)
    series = contract(cross, make_table(width, lag_index))
    bank_float = bank_piece.astype(jnp.float32)
    norm_sum = jnp.sum(bank_float * bank_float, axis=(0, 1))
    series, template_norm = (series, norm_sum)
    power = (
        series[:, :lag_count] * series[:, :lag_count]
        + series[:, lag_count:] * series[:, lag_count:]
    )
    power = power.reshape(count, tpl_rows, lag_count) / template_norm[None, :, None]
    inside = (lag_index[None, :] >= valid_start[:, None]) & (
        lag_index[None, :] < valid_start[:, None] + VALID
    )
    peaks = jnp.max(jnp.where(inside[:, None, :], power, jnp.float32(0.0)), axis=2).T
    return lax.pmax(peaks, "freq")


def solution(mesh):
    in_specs = (P("freq", None, "group"), P("freq", None, "group"), P())
    out_specs = P("group", None)
    return jax.shard_map(
        on_device, mesh=mesh, in_specs=in_specs, out_specs=out_specs, check_vma=False
    )
```

profile of v0, /device:TPU:0, one launch (start us, length us, event | category | flops | bytes accessed | tf_op | source)
XLA Modules:
  0.0 411.2 jit_solution(10462110616772859024)
XLA Ops:
  6.5 2.0 copy.14
  8.5 0.0 all-gather.2.cloned.1.call-update
  8.6 0.7 copy.15
  9.3 6.3 %all_gather.10 = bf16[256,2,16]{0,1,2:T(2,128)(2,1)S(1)} all-gather(bf16[256,2,4]{0,1,2:T(2,128)(2,1)S(1)} %copy.15), channel_id=1, replica_groups=mesh['group'=4,'freq'=8] {'group'}, dimensions={2}, use_global_device_ids=true | all-gather | bytes 20480 | tf_op jit(solution)/shard_map/all_gather | solution.py:44
  15.5 23.8 %all_gather.11 = bf16[2048,2,16]{0,1,2:T(2,128)(2,1)S(1)} all-gather(bf16[256,2,16]{0,1,2:T(2,128)(2,1)S(1)} %all_gather.10), channel_id=1, replica_groups=mesh['group'=4,'freq'=8] {'freq'}, dimensions={0}, use_global_device_ids=true | all-gather | bytes 147456 | tf_op jit(solution)/shard_map/all_gather | solution.py:47
  39.3 0.2 slice_convert_fusion.1
  39.5 0.3 copy.18
  39.9 0.3 copy.19
  40.2 0.7 broadcast_add_fusion
  40.9 0.7 compare_and_fusion
  41.6 0.2 copy.13
  41.8 2.8 broadcast_in_dim.10
  44.6 5.5 %copy.20 = pred[64,8,16,640]{3,1,2,0:T(8,128)(4,1)} copy(pred[64,8,16,640]{3,2,1,0:T(8,128)(4,1)S(1)} %bitcast.22) | data formatting | bytes 10485760
  50.2 18.7 %fusion.21 = (bf16[2048,512]{1,0:T(8,128)(2,1)}, bf16[2048,512]{1,0:T(8,128)(2,1)}, bf16[2048,512]{1,0:T(8,128)(2,1)}) fusion(s32[512]{0:T(512)S(1)} %iota_add_fusion), kind=kLoop, calls=%fused_computation.34 | loop fusion | flops 18874368 | bytes 6293504 | tf_op jit(solution)/shard_map/convert.9
  68.8 30.4 %all-gather.2.cloned.1.call-done = bf16[2048,2,640]{2,0,1:T(8,128)(2,1)} async-done(((bf16[256,2,640]{2,0,1:T(8,128)(2,1)}), bf16[2048,2,640]{2,0,1:T(8,128)(2,1)}) %all-gather.2.cloned.1.call-update) | async-done | bytes 5242896 | tf_op jit(solution)/shard_map/all_gather | solution.py:46
  99.2 7.2 %fusion.19 = (f32[2048,640]{1,0:T(8,128)}, f32[2048,640]{1,0:T(8,128)}) fusion(bf16[2048,2,640]{2,0,1:T(8,128)(2,1)} %all-gather.2.cloned.1.call-done), kind=kLoop, calls=%fused_computation.32 | loop fusion | flops 2621440 | bytes 15728640 | tf_op jit(solution)/shard_map/mul | solution.py:27
  106.4 31.5 %add_convert_fusion = (bf16[1,2048,16,640]{3,2,1,0:T(8,128)(2,1)}, bf16[1,2048,16,640]{3,2,1,0:T(8,128)(2,1)}) fusion(f32[2048,16]{1,0:T(8,128)S(1)} %bitcast.25, f32[2048,640]{1,0:T(8,128)} %get-tuple-element.8, f32[2048,16]{1,0:T(8,128)S(1)} %bitcast.24, f32[2048,640]{1,0:T(8,128)} %get-tuple-element.7), kind=kLoop, calls=%fused_computation.2 | loop fusion | flops 167772160 | bytes 94633984 | tf_op jit(solution)/shard_map/convert.10
  137.9 56.2 %pad_maximum_fusion = bf16[2,2048,16,640]{3,2,1,0:T(8,128)(2,1)} fusion(bf16[1,2048,16,640]{3,2,1,0:T(8,128)(2,1)} %get-tuple-element.6, bf16[1,2048,16,640]{3,2,1,0:T(8,128)(2,1)} %get-tuple-element.5), kind=kLoop, calls=%fused_computation | loop fusion | flops 41943040 | bytes 167772160 | tf_op jit(solution)/shard_map/stack | solution.py:29
  194.1 55.4 %copy.21 = bf16[512,8,16,640]{3,1,2,0:T(8,128)(2,1)} copy(bf16[512,8,16,640]{3,2,1,0:T(8,128)(2,1)} %bitcast.12) | data formatting | bytes 167772160
  249.5 3.6 multiply_reduce_fusion
  253.1 0.6 div.14
  253.7 99.3 %fusion.4 = f32[10240,1024]{0,1:T(8,128)} fusion(bf16[4096,10240]{1,0:T(8,128)(2,1)} %bitcast.13, bf16[2048,512]{1,0:T(8,128)(2,1)} %get-tuple-element.13, bf16[2048,512]{1,0:T(8,128)(2,1)} %get-tuple-element.12, bf16[2048,512]{1,0:T(8,128)(2,1)S(1)} %copy-done), kind=kOutput, calls=%fused_computation.10 | convolution fusion | flops 85932900352 | bytes 132120576 | tf_op jit(solution)/shard_map/dot_general | solution.py:34
  353.0 15.9 %fusion.3 = f32[10240]{0:T(1024)S(1)} fusion(pred[10240,512]{0,1:T(8,128)(4,1)} %bitcast.23, f32[10240,1024]{0,1:T(8,128)} %fusion.4, f32[10240]{0:T(1024)S(1)} %copy-done.1), kind=kLoop, calls=%fused_computation.8 | loop fusion | flops 31447040 | bytes 47267840 | tf_op jit(solution)/shard_map/reduce_max | solution.py:62
  369.0 35.3 %pmax.7 = f32[640,16]{0,1:T(8,128)} all-reduce(f32[640,16]{0,1:T(8,128)S(1)} %bitcast.26), channel_id=1, replica_groups=mesh['group'=4,'freq'=8] {'freq'}, use_global_device_ids=true, to_apply=%region_2.3 | all-reduce | flops 10240 | bytes 81920 | tf_op jit(solution)/shard_map/pmax | solution.py:63
  (8 shorter events, 0.0 us)
Async XLA Ops:
  6.5 92.7 %all-gather.2.cloned.1.call-start = ((), (), s32[]{:S(2)}) async-start(), calls=%async_computation | async-start | bytes 5898240 | tf_op jit(solution)/shard_map/all_gather | solution.py:46
  194.1 59.7 %copy-start = (bf16[2048,512]{1,0:T(8,128)(2,1)S(1)}, bf16[2048,512]{1,0:T(8,128)(2,1)}, u32[]{:S(2)}) copy-start(bf16[2048,512]{1,0:T(8,128)(2,1)} %get-tuple-element.11) | copy-start | bytes 6291460
  253.7 99.3 %copy-start.1 = (f32[10240]{0:T(1024)S(1)}, f32[10240]{0:T(1024)}, u32[]{:S(2)}) copy-start(f32[10240]{0:T(1024)} %div.14) | copy-start | bytes 122884
Sparse Core Ops, SparseCore 0:
  9.5 89.6 all-gather.1
where the time goes:
time: 411 us
  other arithmetic  135 us (33%)
  matrix products  99.3 us (24%)
  local copies, waits for them, and re-layouts  68 us (17%)
  blocking collectives  65.4 us (16%)
  waiting for transfers between devices  30.4 us (7%)
  between operations  13.5 us (3%)
    dot_general x1, matrix products, contract(): lax.dot_general(cross, table, (((0,), (0,)), ((), ())), preferred_element...  99.3 us
    unnamed x8, local copies, waits for them, and re-layouts  63.7 us
    another operation x1, other arithmetic, make_cross(): joined = jnp.stack([cross_re, cross_im], 0).astype(jnp.bfloat16)  56.2 us
    another operation x2, other arithmetic  50.2 us
    pmax x1, blocking collectives, on_device(): return lax.pmax(peaks, 'freq')  35.3 us
    all_gather x1, waiting for transfers between devices, on_device(): bank_piece = lax.all_gather(templates, 'freq', axis=0, tiled=True)  30.4 us
    all_gather x1, blocking collectives, on_device(): seg_piece = lax.all_gather(every_segment, 'freq', axis=0, tiled=True)  23.8 us
    reduce_max x1, other arithmetic, on_device(): jnp.max(jnp.where(inside[:, None, :], power, jnp.float32(0.0)), axis=2)  15.9 us
  transfers between devices with their start and end apart: 1, of which 1 were waited for; matrix products, arithmetic and copies ran while one was open for 7% of the time, Pallas kernels for 0%

commit v1 on v0

v1 whole, which is shorter than its diff:
```python
import functools
import math

import jax
import jax.numpy as jnp
import numpy as np
from jax import lax
from jax.experimental import pallas as pl
from jax.experimental.pallas import tpu as pltpu
from jax.sharding import PartitionSpec as P

LANES = 128
RADIX = 16
SUB = 8
SCALE = 1.1328125


def rotation(angle, row_axis, col_axis):
    cosine, sine = np.cos(angle), np.sin(angle)
    top = np.stack([cosine, -sine], col_axis)
    bottom = np.stack([sine, cosine], col_axis)
    return np.stack([top, bottom], row_axis)


def tables(bins):
    lags = 2 * bins
    inner = lags // RADIX
    a = np.arange(bins // RADIX)
    tau1 = np.arange(inner)
    angle = 2.0 * math.pi * ((tau1[:, None] * a[None, :]) % inner) / inner
    first = rotation(angle.reshape(inner // SUB, SUB, a.size), 1, 2)
    first = first.reshape(inner // SUB, 2, SUB, 2 * a.size)
    turn = 2.0 * math.pi * tau1.reshape(inner // SUB, SUB, 1) / lags
    turn = np.stack([np.cos(turn), np.sin(turn)], 0)
    b = np.arange(RADIX)
    angle = 2.0 * math.pi * ((b[:, None] * b[None, :]) % RADIX) / RADIX
    second = rotation(angle, 0, 2) * SCALE
    second = second.reshape(2 * RADIX, 2 * RADIX)
    second = np.kron(second, np.eye(SUB))
    return first.astype(np.float32), turn.astype(np.float32), second.astype(jnp.bfloat16)


def kernel(valid, r_ref, d_ref, base_ref, turn_ref, w2_ref, vs_ref, out_ref, work_ref, w1_ref, dexp_ref, y_ref):
    step = pl.program_id(0)
    width = out_ref.shape[2]
    parts, _, depth2, _ = r_ref.shape
    depth = depth2 // 2
    segs = d_ref.shape[3]
    per_tile = LANES // segs
    half = parts * depth
    rows2, cols2 = w2_ref.shape
    groups = y_ref.shape[0]
    inner = groups * SUB

    @pl.when(step == 0)
    def _():
        work_ref[...] = base_ref[...]

        @pl.loop(0, RADIX)
        def _(b):
            w1_ref[b] = work_ref[...].reshape(w1_ref.shape[1:]).astype(jnp.bfloat16)
            top, bottom = work_ref[:, 0], work_ref[:, 1]
            cosine, sine = turn_ref[0], turn_ref[1]
            work_ref[:, 0] = top * cosine - bottom * sine
            work_ref[:, 1] = bottom * cosine + top * sine

        seg_spread = (
            lax.broadcasted_iota(jnp.int32, (segs, LANES), 0)
            == lax.broadcasted_iota(jnp.int32, (segs, LANES), 1) // per_tile
        ).astype(jnp.bfloat16)

        @pl.loop(0, RADIX)
        def _(b):
            piece = d_ref[:, b].reshape(2 * half, segs)
            dexp_ref[b] = jnp.dot(piece, seg_spread, preferred_element_type=jnp.float32)

    lane = lax.broadcasted_iota(jnp.int32, (LANES, width), 1)
    wanted = step * (width // segs) + (lane // LANES) * per_tile + lane % per_tile
    pick = (lax.broadcasted_iota(jnp.int32, (LANES, width), 0) == wanted).astype(jnp.bfloat16)

    def split(x):
        x = x.reshape(parts, 2, depth, x.shape[1])
        return x[:, 0].reshape(half, -1), x[:, 1].reshape(half, -1)

    def first_stage(b, norm):
        bank = jnp.dot(
            r_ref[:, b].reshape(2 * half, LANES), pick, preferred_element_type=jnp.float32
        )
        h0, h1 = split(bank)
        d0, d1 = split(dexp_ref[b])
        d0 = jnp.concatenate([d0] * (width // LANES), 1)
        d1 = jnp.concatenate([d1] * (width // LANES), 1)
        square = h0 * h0 + h1 * h1
        norm = norm + jnp.sum(square.reshape(half // SUB, SUB, width), 0)
        cross = jnp.concatenate([h0 * d0 + h1 * d1, h0 * d1 - h1 * d0], 0).astype(jnp.bfloat16)
        y = jnp.dot(w1_ref[b], cross, preferred_element_type=jnp.float32)
        y_ref[:, b] = y.astype(jnp.bfloat16).reshape(groups, 2 * SUB, width)
        return norm

    norm = lax.fori_loop(
        0, RADIX, first_stage, jnp.zeros((SUB, width), jnp.float32), unroll=2
    )
    offset = lax.broadcasted_iota(jnp.int32, (SUB, width), 0) - vs_ref[...]
    row = lax.broadcasted_iota(jnp.int32, (RADIX, SUB, width), 0) * inner

    def second_stage(g, best):
        z = jnp.dot(
            w2_ref[...], y_ref[g].reshape(cols2, width), preferred_element_type=jnp.float32
        )
        re, im = z[: rows2 // 2], z[rows2 // 2 :]
        power = (re * re + im * im).reshape(RADIX, SUB, width)
        late = row + (offset + g * SUB)[None]
        inside = (late >= 0) & (late < valid)
        return jnp.maximum(best, jnp.max(jnp.where(inside, power, 0.0), 0))

    best = lax.fori_loop(
        0, groups, second_stage, jnp.zeros((SUB, width), jnp.float32), unroll=4
    )
    norm = jnp.sum(norm, 0, keepdims=True) * (SCALE * SCALE)
    out_ref[0] = jnp.max(best, 0, keepdims=True) / norm


def correlate(received, strain, starts, rows):
    parts, _, depth2, _ = received.shape
    segs = strain.shape[3]
    bins = parts * RADIX * depth2 // 2
    base, turn, second = tables(bins)
    per_tile = LANES // segs
    tiles = -(-rows // per_tile)
    width = 2 * LANES if tiles % 2 == 0 else LANES
    steps = tiles * LANES // width
    starts = jnp.tile(jnp.repeat(starts, per_tile), width // LANES)
    starts = jnp.broadcast_to(starts[None, :], (SUB, width))
    groups = 2 * bins // RADIX // SUB
    whole = pl.BlockSpec(memory_space=pltpu.VMEM)
    out = pl.pallas_call(
        functools.partial(kernel, bins),
        grid=(steps,),
        out_shape=jax.ShapeDtypeStruct((steps, 1, width), jnp.float32),
        in_specs=[whole] * 6,
        out_specs=pl.BlockSpec((1, 1, width), lambda i: (i, 0, 0)),
        scratch_shapes=[
            pltpu.VMEM(base.shape, jnp.float32),
            pltpu.VMEM((RADIX, groups * 2 * SUB, 2 * bins // RADIX), jnp.bfloat16),
            pltpu.VMEM((RADIX, parts * depth2, LANES), jnp.float32),
            pltpu.VMEM((groups, RADIX, 2 * SUB, width), jnp.bfloat16),
        ],
        compiler_params=pltpu.CompilerParams(vmem_limit_bytes=50 * 1024 * 1024),
    )(received, strain, jnp.asarray(base), jnp.asarray(turn), jnp.asarray(second), starts)
    out = out.reshape(tiles, segs, per_tile)
    return out.transpose(0, 2, 1).reshape(tiles * per_tile, segs)[:rows]


def join_parts(pieces, depth):
    if depth % SUB == 0:
        return pieces
    parts, _, _, last = pieces.shape
    pieces = pieces.reshape(parts, RADIX, 2, depth, last).transpose(1, 2, 0, 3, 4)
    return pieces.reshape(1, RADIX, 2 * parts * depth, last)


def on_device(spectra, templates, valid_start):
    parts = lax.axis_size("freq")
    bins_here, _, rows_here = templates.shape
    depth = bins_here // RADIX
    rows = rows_here // parts
    bank = templates.reshape(depth, RADIX, 2, parts, rows).transpose(3, 1, 2, 0, 4)
    bank = jnp.pad(bank, ((0, 0),) * 4 + ((0, LANES - rows),))
    bank = bank.reshape(parts, RADIX, 2 * depth, LANES)
    received = lax.all_to_all(bank, "freq", 0, 0, tiled=True)
    strain = spectra.reshape(depth, RADIX, 2, -1).transpose(1, 2, 0, 3)
    strain = strain.reshape(RADIX, 2 * depth, -1)
    strain = lax.all_gather(strain, ("freq", "group"), axis=0)
    strain = strain.reshape((parts, -1) + strain.shape[1:])
    strain = strain.transpose(0, 2, 3, 1, 4).reshape(parts, RADIX, 2 * depth, -1)
    peaks = correlate(join_parts(received, depth), join_parts(strain, depth), valid_start, rows)
    return lax.all_gather(peaks, "freq", axis=0, tiled=True)


def solution(mesh):
    in_specs = (P("freq", None, "group"), P("freq", None, "group"), P())
    out_specs = P("group", None)
    return jax.shard_map(
        on_device, mesh=mesh, in_specs=in_specs, out_specs=out_specs, check_vma=False
    )
```

time: 411 us -> 139 us (0.34)
  other arithmetic: 135 us -> 0.02 us
  matrix products: 99.3 us -> 0 us
  local copies, waits for them, and re-layouts: 68 us -> 6.99 us
  Pallas kernels: 0 us -> 41 us
  waiting for transfers between devices: 30.4 us -> 0.01 us
  blocking collectives: 65.4 us -> 83.7 us
  between operations: 13.5 us -> 0.09 us
  starting transfers between devices: 0.01 us -> 7.41 us
    another operation x3 -> x0, other arithmetic: 106 us -> none  [the longest x1 56.2 us: make_cross(): joined = jnp.stack([cross_re, cross_im], 0).astype(jnp.bfloat16)]
    dot_general x1 -> x0, matrix products: 99.3 us -> none  [contract(): lax.dot_general(cross, table, (((0,), (0,)), ((), ())), preferred_element...]
    unnamed x8 -> x12, local copies, waits for them, and re-layouts: 63.7 us -> 1.18 us
    all_gather x2, blocking collectives: 30.1 us -> 83.7 us  [the longest x1 53.1 us: on_device(): strain = lax.all_gather(strain, ('freq', 'group'), axis=0)]
    pallas_call x0 -> x1, Pallas kernels: none -> 41 us  [correlate(): pl.pallas_call(functools.partial(kernel, bins), grid=(steps,), out_shape=...]
    pmax x1 -> x0, blocking collectives: 35.3 us -> none  [on_device(): return lax.pmax(peaks, 'freq')]
    all_gather x1 -> x0, waiting for transfers between devices: 30.4 us -> none  [on_device(): bank_piece = lax.all_gather(templates, 'freq', axis=0, tiled=True)]
    reduce_max x1 -> x0, other arithmetic: 15.9 us -> none  [on_device(): jnp.max(jnp.where(inside[:, None, :], power, jnp.float32(0.0)), axis=2)]
  transfers between devices with their start and end apart: 1 -> 1, of which waited for: 1 -> 0; matrix products, arithmetic and copies ran while one was open for 7% -> 1% of each run, Pallas kernels for 0% -> 0%
where the time goes in v1:
time: 139 us
  blocking collectives  83.7 us (60%)
  Pallas kernels  41 us (29%)
  starting transfers between devices  7.41 us (5%)
  local copies, waits for them, and re-layouts  6.99 us (5%)
    all_gather x1, blocking collectives, on_device(): strain = lax.all_gather(strain, ('freq', 'group'), axis=0)  53.1 us
    pallas_call x1, Pallas kernels, correlate(): pl.pallas_call(functools.partial(kernel, bins), grid=(steps,), out_shape=...  41 us
    all_gather x1, blocking collectives, on_device(): return lax.all_gather(peaks, 'freq', axis=0, tiled=True)  30.5 us
    all_to_all x1, starting transfers between devices, on_device(): received = lax.all_to_all(bank, 'freq', 0, 0, tiled=True)  7.41 us
    reshape x2, local copies, waits for them, and re-layouts, on_device(): templates.reshape(depth, RADIX, 2, parts, rows).transpose(3, 1, 2, 0, 4)  3.44 us
  transfers between devices with their start and end apart: 1, of which 0 were waited for; matrix products, arithmetic and copies ran while one was open for 1% of the time, Pallas kernels for 0%

profile of v1, /device:TPU:0, one launch (start us, length us, event | category | flops | bytes accessed | tf_op | source)
XLA Modules:
  0.0 139.2 jit_solution(682104713486654675)
XLA Ops:
  0.0 2.8 %reshape.23 = bf16[16,16,2,8,80]{4,3,2,1,0:T(8,128)(2,1)S(1)} reshape(bf16[256,2,640]{2,1,0:T(2,128)(2,1)} %param.7) | data formatting | bytes 1310720 | tf_op jit(solution)/shard_map/reshape | solution.py:167
  2.8 0.7 copy.25
  3.5 1.2 pad.4
  4.6 0.0 copy-start.3
  4.7 7.4 %all-to-all-start = ((bf16[8,16,32,128]{3,2,1,0:T(8,128)(2,1)}), bf16[8,16,32,128]{3,2,1,0:T(8,128)(2,1)S(1)}, u32[]{:S(2)}, u32[]{:S(2)}) async-start(bf16[8,16,32,128]{3,2,1,0:T(8,128)(2,1)} %bitcast.1), calls=%async_computation | async-start | bytes 2097152 | tf_op jit(solution)/shard_map/all_to_all | solution.py:170
  12.1 0.0 copy-done.3
  12.1 0.1 reshape.25
  12.2 0.1 copy.19
  12.3 0.1 all_gather_reshape.3
  12.4 53.1 %all_gather.6 = bf16[32,16,32,4]{2,1,3,0:T(8,128)(2,1)S(1)} all-gather(bf16[1,16,32,4]{2,1,3,0:T(8,128)(2,1)S(1)} %all_gather_reshape.3), channel_id=1, replica_groups=mesh['group'=4,'freq'=8] {'freq','group'}, dimensions={0}, use_global_device_ids=true | all-gather | bytes 135168 | tf_op jit(solution)/shard_map/all_gather | solution.py:173
  65.5 0.6 copy.20.d_ref
  66.1 0.1 copy-done.4
  66.2 0.1 broadcast_in_dim.10
  66.2 0.1 tile.7
  66.3 0.0 all-to-all-done.r_ref
  66.3 0.2 copy-done
  66.6 0.1 copy-done.1
  66.6 0.0 copy-done.2
  66.7 41.0 %shard_map.64 = f32[5,1,256]{2,1,0:T(1,128)S(1)} custom-call(bf16[8,16,32,128]{3,2,1,0:T(8,128)(2,1)S(1)} %all-to-all-done.r_ref, bf16[8,16,32,16]{3,2,1,0:T(8,128)(2,1)S(1)} %copy.20.d_ref, f32[32,2,8,256]{3,2,1,0:T(8,128)S(1)} %copy-done, f32[2,32,8,1]{3,2,1,0:T(8,128)S(1)} %copy-done.1, bf16[256,256]{1,0:T(8,128)(2,1)S(1)} %copy-done.2, ...), custom_call_target="tpu_custom_call" | custom-call | tf_op jit(solution)/shard_map/pallas_call | solution.py:136
  107.7 0.1 reshape.28
  107.8 0.1 copy.21
  107.9 0.1 copy.22
  107.9 30.5 %all-gather = f32[8,80,16]{1,2,0:T(8,128)S(1)} all-gather(f32[1,80,16]{1,2,0:T(8,128)S(1)} %copy.22), channel_id=1, replica_groups=mesh['group'=4,'freq'=8] {'freq'}, dimensions={0}, use_global_device_ids=true | all-gather | bytes 46080 | tf_op jit(solution)/shard_map/all_gather | solution.py:177
  138.5 0.7 reshape.31
  (8 shorter events, 0.1 us)
Async XLA Ops:
  4.6 7.4 %copy-start.3 = (bf16[256,2,4]{0,2,1:T(4,128)(2,1)S(1)}, bf16[256,2,4]{0,2,1:T(4,128)(2,1)}, u32[]{:S(2)}) copy-start(bf16[256,2,4]{0,2,1:T(4,128)(2,1)} %param.6) | copy-start | bytes 12292
  4.7 61.7 %all-to-all-start = ((bf16[8,16,32,128]{3,2,1,0:T(8,128)(2,1)}), bf16[8,16,32,128]{3,2,1,0:T(8,128)(2,1)S(1)}, u32[]{:S(2)}, u32[]{:S(2)}) async-start(bf16[8,16,32,128]{3,2,1,0:T(8,128)(2,1)} %bitcast.1), calls=%async_computation | async-start | bytes 2097152 | tf_op jit(solution)/shard_map/all_to_all | solution.py:170
  65.5 0.7 copy-start.4
  65.5 1.1 copy-start
  65.5 1.1 copy-start.1
  65.5 1.1 copy-start.2

commit v2 on v1

--- a/solution.py
+++ b/solution.py
@@ -159,22 +159,29 @@
     return pieces.reshape(1, RADIX, 2 * parts * depth, last)
 
 
+def share(piece, axes):
+    count = lax.axis_size(axes)
+    return lax.all_to_all(jnp.broadcast_to(piece[None], (count,) + piece.shape), axes, 0, 0, tiled=True)
+
+
 def on_device(spectra, templates, valid_start):
     parts = lax.axis_size("freq")
     bins_here, _, rows_here = templates.shape
     depth = bins_here // RADIX
     rows = rows_here // parts
     bank = templates.reshape(depth, RADIX, 2, parts, rows).transpose(3, 1, 2, 0, 4)
-    bank = jnp.pad(bank, ((0, 0),) * 4 + ((0, LANES - rows),))
+    strain = share(spectra.reshape(bins_here * 2, -1).T, "group")
+    segs = strain.shape[0] * strain.shape[1]
+    strain = strain.reshape(segs, depth, RADIX, 2).transpose(2, 3, 1, 0)
+    strain = jnp.broadcast_to(strain[None], (parts,) + strain.shape)
+    bank = jnp.concatenate([bank, strain], 4)
+    bank = jnp.pad(bank, ((0, 0),) * 4 + ((0, LANES - rows - segs),))
     bank = bank.reshape(parts, RADIX, 2 * depth, LANES)
     received = lax.all_to_all(bank, "freq", 0, 0, tiled=True)
-    strain = spectra.reshape(depth, RADIX, 2, -1).transpose(1, 2, 0, 3)
-    strain = strain.reshape(RADIX, 2 * depth, -1)
-    strain = lax.all_gather(strain, ("freq", "group"), axis=0)
-    strain = strain.reshape((parts, -1) + strain.shape[1:])
-    strain = strain.transpose(0, 2, 3, 1, 4).reshape(parts, RADIX, 2 * depth, -1)
+    strain = received[..., rows : rows + segs]
     peaks = correlate(join_parts(received, depth), join_parts(strain, depth), valid_start, rows)
-    return lax.all_gather(peaks, "freq", axis=0, tiled=True)
+    peaks = share(peaks.reshape(1, -1), "freq")
+    return peaks.reshape(rows_here, -1)
 
 
 def solution(mesh):

time: 139 us -> 98 us (0.71)
  blocking collectives: 83.7 us -> 10.2 us
  waiting for transfers between devices: 0.01 us -> 26.2 us
  starting transfers between devices: 7.41 us -> 10.6 us
  other arithmetic: 0.02 us -> 1.82 us
    all_gather x2 -> x0, blocking collectives: 83.7 us -> none  [the longest x1 53.1 us: on_device(): strain = lax.all_gather(strain, ('freq', 'group'), axis=0)]
    all_to_all x1, waiting for transfers between devices: 0.01 us -> 25.8 us  [on_device(): received = lax.all_to_all(bank, 'freq', 0, 0, tiled=True)]
    all_to_all x0 -> x1, blocking collectives: none -> 10.2 us  [share(): lax.all_to_all(jnp.broadcast_to(piece[None], (count,) + piece.shape), axe...]
    all_to_all x0 -> x1, starting transfers between devices: none -> 4.26 us  [share(): lax.all_to_all(jnp.broadcast_to(piece[None], (count,) + piece.shape), axe...]
    concatenate x0 -> x1, other arithmetic: none -> 1.7 us  [on_device(): bank = jnp.concatenate([bank, strain], 4)]
  transfers between devices with their start and end apart: 1 -> 2, of which waited for: 0 -> 2; matrix products, arithmetic and copies ran while one was open for 1% -> 4% of each run, Pallas kernels for 0% -> 0%
where the time goes in v2:
time: 98 us; the launch traced here: 97.7 us
  Pallas kernels  41 us (42%)
  waiting for transfers between devices  26.2 us (27%)
  starting transfers between devices  10.6 us (11%)
  blocking collectives  10.2 us (10%)
  local copies, waits for them, and re-layouts  7.61 us (8%)
  other arithmetic  1.82 us (2%)
    pallas_call x1, Pallas kernels, correlate(): pl.pallas_call(functools.partial(kernel, bins), grid=(steps,), out_shape=...  41 us
    all_to_all x1, waiting for transfers between devices, on_device(): received = lax.all_to_all(bank, 'freq', 0, 0, tiled=True)  25.8 us
    all_to_all x1, blocking collectives, share(): lax.all_to_all(jnp.broadcast_to(piece[None], (count,) + piece.shape), axe...  10.2 us
    all_to_all x1, starting transfers between devices, on_device(): received = lax.all_to_all(bank, 'freq', 0, 0, tiled=True)  6.37 us
    all_to_all x1, starting transfers between devices, share(): lax.all_to_all(jnp.broadcast_to(piece[None], (count,) + piece.shape), axe...  4.26 us
    reshape x2, local copies, waits for them, and re-layouts, on_device(): templates.reshape(depth, RADIX, 2, parts, rows).transpose(3, 1, 2, 0, 4)  3.44 us
  transfers between devices with their start and end apart: 2, of which 2 were waited for; matrix products, arithmetic and copies ran while one was open for 4% of the time, Pallas kernels for 0%

profile of v2, /device:TPU:0, one launch (start us, length us, event | category | flops | bytes accessed | tf_op | source)
XLA Modules:
  0.0 97.7 jit_solution(6799632850957194110)
XLA Ops:
  0.0 0.9 copy.15
  0.9 0.1 copy.16
  1.0 0.6 broadcast_in_dim.14
  1.6 4.3 %all-to-all-start = ((bf16[4,4,512]{2,1,0:T(4,128)(2,1)}), bf16[4,4,512]{2,1,0:T(4,128)(2,1)S(1)}, u32[]{:S(2)}, u32[]{:S(2)}) async-start(bf16[4,4,512]{2,1,0:T(4,128)(2,1)} %broadcast_in_dim.14), calls=%async_computation | async-start | bytes 32768 | tf_op jit(solution)/shard_map/all_to_all | solution.py:164
  5.9 2.8 %reshape.25 = bf16[16,16,2,8,80]{4,3,2,1,0:T(8,128)(2,1)S(1)} reshape(bf16[256,2,640]{2,1,0:T(2,128)(2,1)} %param.7) | data formatting | bytes 1310720 | tf_op jit(solution)/shard_map/reshape | solution.py:172
  8.6 0.7 copy.22
  9.3 0.4 all-to-all-done
  9.7 0.3 copy.17
  10.1 0.3 reshape.27
  10.4 0.2 broadcast_in_dim.30
  10.6 1.7 %fusion.2 = bf16[8,16,2,16,128]{4,3,2,1,0:T(8,128)(2,1)} fusion(bf16[8,16,2,16,16]{4,3,2,1,0:T(8,128)(2,1)S(1)} %broadcast_in_dim.30, bf16[8,16,2,16,80]{4,3,2,1,0:T(8,128)(2,1)S(1)} %bitcast.13), kind=kLoop, calls=%fused_computation.3 | loop fusion | flops 3670016 | bytes 1835008 | tf_op jit(solution)/shard_map/concatenate | solution.py:177
  12.3 6.4 %all-to-all-start.1 = ((bf16[8,16,32,128]{3,2,1,0:T(8,128)(2,1)}), bf16[8,16,32,128]{3,2,1,0:T(8,128)(2,1)S(1)}, u32[]{:S(2)}, u32[]{:S(2)}) async-start(bf16[8,16,32,128]{3,2,1,0:T(8,128)(2,1)} %bitcast.4), calls=%async_computation.1 | async-start | bytes 2097152 | tf_op jit(solution)/shard_map/all_to_all | solution.py:180
  18.7 0.1 broadcast_in_dim.31
  18.8 0.1 tile.7
  18.9 25.8 %all-to-all-done.1.r_ref = bf16[8,16,32,128]{3,2,1,0:T(8,128)(2,1)S(1)} async-done(((bf16[8,16,32,128]{3,2,1,0:T(8,128)(2,1)}), bf16[8,16,32,128]{3,2,1,0:T(8,128)(2,1)S(1)}, u32[]{:S(2)}, u32[]{:S(2)}) %all-to-all-start.1) | async-done | bytes 1048608 | tf_op jit(solution)/shard_map/all_to_all | solution.py:180
  44.7 0.4 slice.4.d_ref
  45.1 41.0 %shard_map.64 = f32[5,1,256]{2,1,0:T(1,128)S(1)} custom-call(bf16[8,16,32,128]{3,2,1,0:T(8,128)(2,1)S(1)} %all-to-all-done.1.r_ref, bf16[8,16,32,16]{3,2,1,0:T(8,128)(2,1)S(1)} %slice.4.d_ref, f32[32,2,8,256]{3,2,1,0:T(8,128)S(1)} %copy-done, f32[2,32,8,1]{3,2,1,0:T(8,128)S(1)} %copy-done.1, bf16[256,256]{1,0:T(8,128)(2,1)S(1)} %copy-done.2, ...), custom_call_target="tpu_custom_call" | custom-call | tf_op jit(solution)/shard_map/pallas_call | solution.py:136
  86.2 0.1 reshape.29
  86.3 0.1 copy.19
  86.3 0.1 broadcast_in_dim.34
  86.5 10.2 %all_to_all.15 = f32[8,1,1280]{2,1,0:T(1,128)S(1)} all-to-all(f32[8,1,1280]{2,1,0:T(1,128)S(1)} %broadcast_in_dim.35), channel_id=1, replica_groups=mesh['group'=4,'freq'=8] {'freq'}, dimensions={0} | all-to-all | bytes 81920 | tf_op jit(solution)/shard_map/all_to_all | solution.py:164
  96.6 0.1 reduce.1
  96.7 0.1 reshape.30
  96.9 0.8 copy.20
  (13 shorter events, 0.1 us)
Async XLA Ops:
  1.6 8.1 %all-to-all-start = ((bf16[4,4,512]{2,1,0:T(4,128)(2,1)}), bf16[4,4,512]{2,1,0:T(4,128)(2,1)S(1)}, u32[]{:S(2)}, u32[]{:S(2)}) async-start(bf16[4,4,512]{2,1,0:T(4,128)(2,1)} %broadcast_in_dim.14), calls=%async_computation | async-start | bytes 32768 | tf_op jit(solution)/shard_map/all_to_all | solution.py:164
  12.3 6.4 %copy-start.3 = (s32[16]{0:T(128)S(1)}, s32[16]{0:T(128)}, u32[]{:S(2)}) copy-start(s32[16]{0:T(128)} %param.8) | copy-start | bytes 196
  12.3 32.4 %all-to-all-start.1 = ((bf16[8,16,32,128]{3,2,1,0:T(8,128)(2,1)}), bf16[8,16,32,128]{3,2,1,0:T(8,128)(2,1)S(1)}, u32[]{:S(2)}, u32[]{:S(2)}) async-start(bf16[8,16,32,128]{3,2,1,0:T(8,128)(2,1)} %bitcast.4), calls=%async_computation.1 | async-start | bytes 2097152 | tf_op jit(solution)/shard_map/all_to_all | solution.py:180
  18.9 26.2 %copy-start = (f32[32,2,8,256]{3,2,1,0:T(8,128)S(1)}, f32[32,2,8,256]{3,2,1,0:T(8,128)}, u32[]{:S(2)}) copy-start(f32[32,2,8,256]{3,2,1,0:T(8,128)} %constant.9.clone.base_ref) | copy-start | bytes 1572868
  18.9 26.2 %copy-start.1 = (f32[2,32,8,1]{3,2,1,0:T(8,128)S(1)}, f32[2,32,8,1]{3,2,1,0:T(8,128)}, u32[]{:S(2)}) copy-start(f32[2,32,8,1]{3,2,1,0:T(8,128)} %constant.10.clone.turn_ref) | copy-start | bytes 6148
  18.9 26.2 %copy-start.2 = (bf16[256,256]{1,0:T(8,128)(2,1)S(1)}, bf16[256,256]{1,0:T(8,128)(2,1)}, u32[]{:S(2)}) copy-start(bf16[256,256]{1,0:T(8,128)(2,1)} %constant.11.clone.w2_ref) | copy-start | bytes 393220
